TPU v7x, 32 devices: a whole 2x2x4 slice. The times are simulated.
32 devices in a mesh: batch: 8 (over z, x), mp: 4 (over y, core).
Axes of the slice: x: 2, y: 2, z: 4, core: 2. Of those that a mesh axis runs over, the one named last changes fastest.
Arguments:
- tokens: bfloat16 [16, 2048, 768], P('batch', 'mp'), may hold values from -6 to 6
- cotangent: bfloat16 [16, 2048, 768], P('batch', 'mp'), may hold values from -6 to 6
- lengths: int32 [16], P('batch'), may hold values from 64 to 2048, as said below
- pre_attn_gain: bfloat16 [768], replicated, may hold values from 0.099609375 to 1.8984375
- pre_attn_bias: bfloat16 [768], replicated, may hold values from -3 to 3
- qkv_weight: bfloat16 [3, 768, 768], replicated, may hold values from -0.21875 to 0.21875
- conv_weight: bfloat16 [3, 3, 768], replicated, may hold values from -3 to 3
- out_weight: bfloat16 [768, 768], replicated, may hold values from -1.5 to 1.5
- pre_ffn_gain: bfloat16 [768], replicated, may hold values from 0.099609375 to 1.8984375
- pre_ffn_bias: bfloat16 [768], replicated, may hold values from -3 to 3
- up_weight: bfloat16 [768, 3072], replicated, may hold values from -0.21875 to 0.21875
- up_bias: bfloat16 [3072], replicated, may hold values from -3 to 3
- down_weight: bfloat16 [3072, 768], replicated, may hold values from -0.109375 to 0.109375
- down_bias: bfloat16 [768], replicated, may hold values from -3 to 3
Outputs:
- output: bfloat16 [16, 2048, 768], P('batch', 'mp')
- tokens_grad: bfloat16 [16, 2048, 768], P('batch', 'mp')
- pre_attn_gain_grad: float32 [768], P(('batch', 'mp'))
- pre_attn_bias_grad: float32 [768], P(('batch', 'mp'))
- qkv_weight_grad: float32 [3, 768, 768], P(None, 'batch', 'mp')
- conv_weight_grad: float32 [3, 3, 768], P(None, None, ('batch', 'mp'))
- out_weight_grad: float32 [768, 768], P(('batch', 'mp'))
- pre_ffn_gain_grad: float32 [768], P(('batch', 'mp'))
- pre_ffn_bias_grad: float32 [768], P(('batch', 'mp'))
- up_weight_grad: float32 [768, 3072], P(('batch', 'mp'))
- up_bias_grad: float32 [3072], P(('batch', 'mp'))
- down_weight_grad: float32 [3072, 768], P(('batch', 'mp'))
- down_bias_grad: float32 [768], P(('batch', 'mp'))
Inputs may be any that keep to these rules, and one draw needn't show every extreme that they name: `lengths`: real tokens of each sequence; positions at or past it are padding. Some sequence has 2048 in every draw.
All inputs are finite; a program needn't handle non-finite values.
Results may differ from a plain program's by a relative error of at most 0.014.
The roundings to bfloat16 on the way count: a program that leaves them out, or rounds other values in their place, can miss the bound.
Values may be sent and summed in bfloat16 or wider, within the bound.
No kernel may reach another device: no remote copies, remote signals or barrier semaphores. Data moves between devices by JAX's collectives and lax.ppermute only.
A program may use at most 320 MiB of HBM per device.

v0:
```python
import jax
import jax.numpy as jnp
from jax import lax
from jax.sharding import PartitionSpec as P

HEAD_DIM = 64
QBLOCK = 512
EPSILON = 1e-05
NEGATIVE = -1000000000.0


def norm_forward(values, norm_gain, offset):
    center = values - jnp.mean(values, axis=-1, keepdims=True)
    inv_std = lax.rsqrt(jnp.mean(center * center, axis=-1, keepdims=True) + EPSILON)
    scaled = center * inv_std
    return (scaled * norm_gain + offset, scaled, inv_std)


def norm_backward(grad_out, norm_gain, scaled, inv_std):
    weighted = grad_out * norm_gain
    return inv_std * (
        weighted
        - jnp.mean(weighted, axis=-1, keepdims=True)
        - scaled * jnp.mean(weighted * scaled, axis=-1, keepdims=True)
    )


def conv_forward(values, kernel):
    taps = kernel.shape[1]
    seq_len = values.shape[0]
    padded = jnp.pad(values, ((taps - 1, 0), (0, 0), (0, 0)))
    total_sum = jnp.zeros(values.shape, jnp.float32)
    for offset in range(taps):
        first = taps - 1 - offset
        total_sum = total_sum + kernel[:, offset, :] * padded[first : first + seq_len]
    return (total_sum, padded)


def conv_backward(grad_mixed, kernel, padded):
    taps = kernel.shape[1]
    seq_len = grad_mixed.shape[0]
    grad_padded = jnp.pad(grad_mixed, ((0, taps - 1), (0, 0), (0, 0)))
    grad_values = jnp.zeros(grad_mixed.shape, jnp.float32)
    kernel_grads = []
    for offset in range(taps):
        first = taps - 1 - offset
        grad_values = grad_values + kernel[:, offset, :] * grad_padded[offset : offset + seq_len]
        kernel_grads.append(jnp.sum(grad_mixed * padded[first : first + seq_len], axis=0))
    return (grad_values, jnp.stack(kernel_grads, axis=1))


def block_scores(block_q, key_heads, first, length, key_pos):
    scores = jnp.einsum(
        "qhd,khd->hqk", block_q, key_heads, preferred_element_type=jnp.float32
    ) * HEAD_DIM ** (-0.5)
    query_pos = first + jnp.arange(block_q.shape[0], dtype=jnp.int32)
    allowed = (key_pos[None, :] <= query_pos[:, None]) & (key_pos[None, :] < length)
    return jnp.where(allowed[None], scores, NEGATIVE)


def attend_forward(mixed_b, length):
    seq_len = mixed_b.shape[0]
    head_vals = mixed_b.reshape(seq_len, 3, -1, HEAD_DIM)
    queries = head_vals[:, 0]
    key_heads = head_vals[:, 1]
    values = head_vals[:, 2]
    key_pos = jnp.arange(seq_len, dtype=jnp.int32)
    out_parts = []
    log_totals = []
    for first in range(0, seq_len, QBLOCK):
        scores = block_scores(queries[first : first + QBLOCK], key_heads, first, length, key_pos)
        log_total = jax.nn.logsumexp(scores, axis=-1, keepdims=True)
        prob_block = jnp.exp(scores - log_total).astype(jnp.bfloat16)
        out_parts.append(
            jnp.einsum("hqk,khd->qhd", prob_block, values, preferred_element_type=jnp.float32)
        )
        log_totals.append(log_total)
    return (jnp.concatenate(out_parts, axis=0).reshape(seq_len, -1), log_totals)


def attend_backward(mixed_b, grad_heads, log_totals, length):
    seq_len = mixed_b.shape[0]
    head_vals = mixed_b.reshape(seq_len, 3, -1, HEAD_DIM)
    queries = head_vals[:, 0]
    key_heads = head_vals[:, 1]
    values = head_vals[:, 2]
    grad_out = grad_heads.reshape(seq_len, -1, HEAD_DIM)
    key_pos = jnp.arange(seq_len, dtype=jnp.int32)
    scale = HEAD_DIM ** (-0.5)
    query_parts = []
    grad_keys = jnp.zeros(key_heads.shape, jnp.float32)
    grad_values = jnp.zeros(values.shape, jnp.float32)
    for block_index, first in enumerate(range(0, seq_len, QBLOCK)):
        block_q = queries[first : first + QBLOCK]
        scores = block_scores(block_q, key_heads, first, length, key_pos)
        prob_block = jnp.exp(scores - log_totals[block_index])
        block_grad = grad_out[first : first + QBLOCK]
        grad_values = grad_values + jnp.einsum(
            "hqk,qhd->khd",
            prob_block.astype(jnp.bfloat16),
            block_grad,
            preferred_element_type=jnp.float32,
        )
        grad_probs = jnp.einsum(
            "qhd,khd->hqk", block_grad, values, preferred_element_type=jnp.float32
        )
        row_delta = jnp.sum(grad_probs * prob_block, axis=-1, keepdims=True)
        grad_scores = (prob_block * (grad_probs - row_delta)).astype(jnp.bfloat16)
        query_parts.append(
            jnp.einsum("hqk,khd->qhd", grad_scores, key_heads, preferred_element_type=jnp.float32)
            * scale
        )
        grad_keys = (
            grad_keys
            + jnp.einsum("hqk,qhd->khd", grad_scores, block_q, preferred_element_type=jnp.float32)
            * scale
        )
    grad_queries = jnp.concatenate(query_parts, axis=0)
    return jnp.stack([grad_queries, grad_keys, grad_values], axis=1).reshape(seq_len, 3, -1)


def on_device(
    tokens,
    cotangent,
    lengths,
    pre_attn_gain,
    pre_attn_bias,
    qkv_weight,
    conv_weight,
    out_weight,
    pre_ffn_gain,
    pre_ffn_bias,
    up_weight,
    up_bias,
    down_weight,
    down_bias,
):
    groups = lax.axis_size("mp")
    member = lax.axis_index("mp")
    batch_groups = lax.axis_size("batch")
    local_rows = tokens.shape[1]
    model_width = tokens.shape[2]
    head_cols = model_width // groups
    col_start = member * head_cols
    taps = conv_weight.shape[1]
    kernel_own = lax.dynamic_slice_in_dim(conv_weight, col_start, head_cols, 2).astype(jnp.float32)
    gain_attn = pre_attn_gain.astype(jnp.float32)
    bias_attn = pre_attn_bias.astype(jnp.float32)
    gain_ffn = pre_ffn_gain.astype(jnp.float32)
    bias_ffn = pre_ffn_bias.astype(jnp.float32)
    up_bias_f = up_bias.astype(jnp.float32)
    down_bias_f = down_bias.astype(jnp.float32)
    row_pos = member * local_rows + jnp.arange(local_rows, dtype=jnp.int32)
    qkv_grad_shape = (3, model_width, model_width)

    def one_batch(running, inputs):
        seq_rows, grad_rows, length = inputs
        rows_f = seq_rows.astype(jnp.float32)
        valid_rows = (row_pos < length)[:, None]
        normed, scaled_attn, inv_attn = norm_forward(rows_f, gain_attn, bias_attn)
        normed_b = normed.astype(jnp.bfloat16)
        local_proj = jnp.einsum(
            "td,cde->tce", normed_b, qkv_weight, preferred_element_type=jnp.float32
        ).astype(jnp.bfloat16)
        projected_b = lax.all_to_all(local_proj, "mp", split_axis=2, concat_axis=0, tiled=True)
        mixed_f, padded = conv_forward(projected_b.astype(jnp.float32), kernel_own)
        mixed_b = mixed_f.astype(jnp.bfloat16)
        heads_out, log_totals = attend_forward(mixed_b, length)
        heads_tok = lax.all_to_all(
            heads_out.astype(jnp.bfloat16), "mp", split_axis=0, concat_axis=1, tiled=True
        )
        attended = jnp.dot(heads_tok, out_weight, preferred_element_type=jnp.float32)
        residual = rows_f + attended
        normed_ffn, scaled_ffn, inv_ffn = norm_forward(residual, gain_ffn, bias_ffn)
        normed_ffn_b = normed_ffn.astype(jnp.bfloat16)
        hidden_pre = (
            jnp.dot(normed_ffn_b, up_weight, preferred_element_type=jnp.float32) + up_bias_f
        )
        relu_part = jnp.maximum(hidden_pre, 0.0)
        activated = jnp.square(relu_part).astype(jnp.bfloat16)
        ffn_out = jnp.dot(activated, down_weight, preferred_element_type=jnp.float32) + down_bias_f
        result = jnp.where(valid_rows, residual + ffn_out, 0.0).astype(jnp.bfloat16)
        grad_y = jnp.where(valid_rows, grad_rows.astype(jnp.float32), 0.0)
        grad_ffn = grad_y.astype(jnp.bfloat16)
        grad_down = jnp.einsum("tf,td->fd", activated, grad_ffn, preferred_element_type=jnp.float32)
        grad_down_bias = jnp.sum(grad_ffn.astype(jnp.float32), axis=0)
        grad_act = jnp.einsum(
            "td,fd->tf", grad_ffn, down_weight, preferred_element_type=jnp.float32
        )
        grad_pre = (2.0 * relu_part * grad_act).astype(jnp.bfloat16)
        grad_up = jnp.einsum(
            "td,tf->df", normed_ffn_b, grad_pre, preferred_element_type=jnp.float32
        )
        grad_up_bias = jnp.sum(grad_pre.astype(jnp.float32), axis=0)
        grad_normed_ffn = jnp.einsum(
            "tf,df->td", grad_pre, up_weight, preferred_element_type=jnp.float32
        )
        grad_gain_ffn = jnp.sum(grad_normed_ffn * scaled_ffn, axis=0)
        grad_bias_ffn = jnp.sum(grad_normed_ffn, axis=0)
        grad_residual = grad_y + norm_backward(grad_normed_ffn, gain_ffn, scaled_ffn, inv_ffn)
        grad_attended = grad_residual.astype(jnp.bfloat16)
        grad_out_w = jnp.einsum(
            "te,td->ed", heads_tok, grad_attended, preferred_element_type=jnp.float32
        )
        grad_heads_tok = jnp.einsum(
            "td,ed->te", grad_attended, out_weight, preferred_element_type=jnp.float32
        ).astype(jnp.bfloat16)
        grad_heads = lax.all_to_all(grad_heads_tok, "mp", split_axis=1, concat_axis=0, tiled=True)
        grad_mixed = attend_backward(mixed_b, grad_heads, log_totals, length)
        grad_proj, grad_conv = conv_backward(grad_mixed, kernel_own, padded)
        grad_proj_b = grad_proj.astype(jnp.bfloat16)
        grad_proj_tok = lax.all_to_all(grad_proj_b, "mp", split_axis=0, concat_axis=2, tiled=True)
        grad_qkv = jnp.einsum(
            "td,tce->cde", normed_b, grad_proj_tok, preferred_element_type=jnp.float32
        )
        grad_normed = jnp.einsum(
            "tce,cde->td", grad_proj_tok, qkv_weight, preferred_element_type=jnp.float32
        )
        grad_gain_attn = jnp.sum(grad_normed * scaled_attn, axis=0)
        grad_bias_attn = jnp.sum(grad_normed, axis=0)
        grad_tokens = grad_residual + norm_backward(grad_normed, gain_attn, scaled_attn, inv_attn)
        updates = (
            grad_gain_attn,
            grad_bias_attn,
            grad_qkv,
            grad_conv,
            grad_out_w,
            grad_gain_ffn,
            grad_bias_ffn,
            grad_up,
            grad_up_bias,
            grad_down,
            grad_down_bias,
        )
        running = jax.tree.map(jnp.add, running, updates)
        return (running, (result, grad_tokens.astype(jnp.bfloat16)))

    start_grads = (
        jnp.zeros((model_width,), jnp.float32),
        jnp.zeros((model_width,), jnp.float32),
        jnp.zeros(qkv_grad_shape, jnp.float32),
        jnp.zeros((3, taps, head_cols), jnp.float32),
        jnp.zeros(out_weight.shape, jnp.float32),
        jnp.zeros((model_width,), jnp.float32),
        jnp.zeros((model_width,), jnp.float32),
        jnp.zeros(up_weight.shape, jnp.float32),
        jnp.zeros(up_bias.shape, jnp.float32),
        jnp.zeros(down_weight.shape, jnp.float32),
        jnp.zeros((model_width,), jnp.float32),
    )
    running, outputs = lax.scan(one_batch, start_grads, (tokens, cotangent, lengths))
    conv_full = lax.dynamic_update_slice_in_dim(
        jnp.zeros((3, taps, model_width), jnp.float32), running[3], col_start, 2
    )
    rows_part = model_width // batch_groups
    qkv_flat = (
        running[2]
        .reshape(3, batch_groups, rows_part, groups, head_cols)
        .transpose(1, 3, 0, 2, 4)
        .reshape(batch_groups * groups * 3 * rows_part, head_cols)
    )
    summed = (
        lax.psum_scatter(running[0], ("batch", "mp"), scatter_dimension=0, tiled=True),
        lax.psum_scatter(running[1], ("batch", "mp"), scatter_dimension=0, tiled=True),
        lax.psum_scatter(qkv_flat, ("batch", "mp"), scatter_dimension=0, tiled=True),
        lax.psum_scatter(conv_full, ("batch", "mp"), scatter_dimension=2, tiled=True),
        lax.psum_scatter(running[4], ("batch", "mp"), scatter_dimension=0, tiled=True),
        lax.psum_scatter(running[5], ("batch", "mp"), scatter_dimension=0, tiled=True),
        lax.psum_scatter(running[6], ("batch", "mp"), scatter_dimension=0, tiled=True),
        lax.psum_scatter(running[7], ("batch", "mp"), scatter_dimension=0, tiled=True),
        lax.psum_scatter(running[8], ("batch", "mp"), scatter_dimension=0, tiled=True),
        lax.psum_scatter(running[9], ("batch", "mp"), scatter_dimension=0, tiled=True),
        lax.psum_scatter(running[10], ("batch", "mp"), scatter_dimension=0, tiled=True),
    )
    qkv_sum = summed[2].reshape(3, rows_part, head_cols)
    return (
        outputs[0],
        outputs[1],
        summed[0],
        summed[1],
        qkv_sum,
        summed[3],
        summed[4],
        summed[5],
        summed[6],
        summed[7],
        summed[8],
        summed[9],
        summed[10],
    )


def solution(mesh):
    in_specs = (
        P("batch", "mp", None),
        P("batch", "mp", None),
        P("batch"),
        P(),
        P(),
        P(),
        P(),
        P(),
        P(),
        P(),
        P(),
        P(),
        P(),
        P(),
    )
    out_specs = (
        P("batch", "mp", None),
        P("batch", "mp", None),
        P(("batch", "mp")),
        P(("batch", "mp")),
        P(None, "batch", "mp"),
        P(None, None, ("batch", "mp")),
        P(("batch", "mp"), None),
        P(("batch", "mp")),
        P(("batch", "mp")),
        P(("batch", "mp"), None),
        P(("batch", "mp")),
        P(("batch", "mp"), None),
        P(("batch", "mp")),
    )
    return jax.shard_map(
        on_device, mesh=mesh, in_specs=in_specs, out_specs=out_specs, check_vma=False
    )
```

profile of v0, /device:TPU:0, one launch (start us, length us, event | category | flops | bytes accessed | tf_op | source)
XLA Modules:
  0.0 1405.1 jit_solution(3746548389037983586)
XLA Ops:
  13.4 859.4 %while.37 = (s32[]{:T(128)}, f32[768]{0:T(1024)}, f32[768]{0:T(1024)}, f32[3,768,768]{1,2,0:T(8,128)}, f32[3,3,192]{2,1,0:T(4,128)}, /*index=5*/f32[768,768]{1,0...) while((s32[]{:T(128)}, f32[768]{0:T(1024)}, ...), condition=%wide.region_30.31_spmd.clone, body=%wide.region_0.30_spmd.clone.sunk | while | flops 31852625920 | bytes 1296953600 | solution.py:251
  37.0 30.4 %all-to-all-done = bf16[512,3,768]{0,1,2:T(4,128)(2,1)} async-done(((bf16[512,3,768]{0,1,2:T(4,128)(2,1)}), bf16[512,3,768]{0,1,2:T(4,128)(2,1)}, u32[]{:S(2)}, u32[]{:S(2)}) %all-to-all-start) | async-done | bytes 2359328 | tf_op jit(solution)/shard_map/while/body/eval_jaxpr/all_to_all | solution.py:165
  141.9 6.8 exponential_reduce_fusion.8
  161.4 10.9 all-to-all-done.1
  180.9 7.7 convert_reduce_fusion.7
  201.8 7.8 fusion.265
  219.6 7.8 fusion.255
  227.4 11.6 multiply_reduce_fusion.19
  239.1 8.8 multiply_convert_fusion.16
  255.3 8.9 multiply_reduce_fusion.20
  264.2 6.9 convolution_add_fusion.11
  271.1 9.3 multiply_reduce_fusion.21
  287.0 10.3 multiply_reduce_fusion.22
  297.3 8.4 convolution_add_fusion.13
  305.7 9.8 multiply_convert_fusion.19
  318.3 9.9 multiply_convert_fusion.18
  333.9 7.0 multiply_convert_fusion.17
  357.8 7.0 copy.98
  370.1 9.5 select_add_fusion.22
  392.6 25.7 %all-to-all-done.3 = bf16[2048,3,192]{2,1,0:T(4,128)(2,1)} async-done(((bf16[2048,3,192]{2,1,0:T(4,128)(2,1)}), bf16[2048,3,192]{2,1,0:T(4,128)(2,1)}, u32[]{:S(2)}, u32[]{:S(2)}) %all-to-all-start.3) | async-done | bytes 2359328 | tf_op jit(solution)/shard_map/while/body/eval_jaxpr/all_to_all | solution.py:212
  418.3 7.4 copy.99
  463.4 29.8 %all-to-all-done = bf16[512,3,768]{0,1,2:T(4,128)(2,1)} async-done(((bf16[512,3,768]{0,1,2:T(4,128)(2,1)}), bf16[512,3,768]{0,1,2:T(4,128)(2,1)}, u32[]{:S(2)}, u32[]{:S(2)}) %all-to-all-start) | async-done | bytes 2359328 | tf_op jit(solution)/shard_map/while/body/eval_jaxpr/all_to_all | solution.py:165
  587.2 10.9 all-to-all-done.1
  606.8 7.7 convert_reduce_fusion.7
  627.7 7.8 fusion.265
  635.5 8.0 select_add_fusion.20
  649.5 7.8 fusion.255
  657.4 11.6 multiply_reduce_fusion.19
  669.0 8.8 multiply_convert_fusion.16
  685.3 8.9 multiply_reduce_fusion.20
  694.2 6.9 convolution_add_fusion.11
  701.1 9.3 multiply_reduce_fusion.21
  716.9 10.3 multiply_reduce_fusion.22
  727.3 8.4 convolution_add_fusion.13
  735.7 9.8 multiply_convert_fusion.19
  748.3 9.9 multiply_convert_fusion.18
  763.9 7.0 multiply_convert_fusion.17
  787.8 7.0 copy.98
  800.1 12.3 select_add_fusion.22
  825.3 22.9 %all-to-all-done.3 = bf16[2048,3,192]{2,1,0:T(4,128)(2,1)} async-done(((bf16[2048,3,192]{2,1,0:T(4,128)(2,1)}), bf16[2048,3,192]{2,1,0:T(4,128)(2,1)}, u32[]{:S(2)}, u32[]{:S(2)}) %all-to-all-start.3) | async-done | bytes 2359328 | tf_op jit(solution)/shard_map/while/body/eval_jaxpr/all_to_all | solution.py:212
  848.2 7.4 copy.99
  872.9 10.4 reshape.455
  883.3 10.2 copy.74
  895.2 41.7 %all-reduce.9 = (f32[768]{0:T(1024)S(1)}, f32[768]{0:T(1024)S(1)}, f32[3,3,768]{2,1,0:T(4,128)S(1)}, f32[768]{0:T(1024)S(1)}, f32[768]{0:T(1024)S(1)}, /*index=5*/f32[3072]{0:T(1024)S(1)}, f32[768]{0:T(1024)S(1)}) all-reduce(f32[768]{0:T(1024)S(1)} %copy-done.70, ...), channel_id=2, replica_groups=mesh['batch'=8,'mp'=4] {'batch','mp'}, use_global_device_ids=true, to_apply=%region_31.32.clone | all-reduce | flops 13824 | bytes 110592
  941.1 32.0 %reduce-scatter.8.cloned.1.call-done = f32[24,768]{1,0:T(8,128)} async-done(((f32[768,768]{1,0:T(8,128)}), f32[24,768]{1,0:T(8,128)}) %reduce-scatter.8.cloned.1.call-update) | async-done | bytes 73744 | tf_op jit(solution)/shard_map/reduce_scatter | solution.py:267
  973.1 142.0 %reduce-scatter.6.cloned.1.call-done = f32[288,192]{1,0:T(8,128)} async-done(((f32[9216,192]{1,0:T(8,128)}), f32[288,192]{1,0:T(8,128)}) %reduce-scatter.6.cloned.1.call-update) | async-done | bytes 221200 | tf_op jit(solution)/shard_map/reduce_scatter | solution.py:265
  1115.1 141.1 %reduce-scatter.10.cloned.1.call-done = f32[24,3072]{1,0:T(8,128)} async-done(((f32[768,3072]{1,0:T(8,128)}), f32[24,3072]{1,0:T(8,128)}) %reduce-scatter.10.cloned.1.call-update) | async-done | bytes 294928 | tf_op jit(solution)/shard_map/reduce_scatter | solution.py:270
  1256.3 142.0 %reduce-scatter.12.cloned.1.call-done = f32[96,768]{1,0:T(8,128)} async-done(((f32[3072,768]{1,0:T(8,128)}), f32[96,768]{1,0:T(8,128)}) %reduce-scatter.12.cloned.1.call-update) | async-done | bytes 294928 | tf_op jit(solution)/shard_map/reduce_scatter | solution.py:272
  (596 shorter events, 440.2 us)
Async XLA Ops:
  7.2 965.9 %reduce-scatter.8.cloned.1.call-start = ((), (), s32[]{:S(2)}) async-start(), calls=%async_computation.9 | async-start | bytes 2433024 | tf_op jit(solution)/shard_map/reduce_scatter | solution.py:267
  13.4 188.4 %copy-start.72 = (f32[768]{0:T(1024)}, f32[768]{0:T(1024)S(1)}, u32[]{:S(2)}) copy-start(f32[768]{0:T(1024)S(1)} %get-tuple-element.969) | copy-start | bytes 9220 | tf_op jit(solution)/shard_map/while
  13.4 196.3 %copy-start.37 = (f32[768]{0:T(1024)}, f32[768]{0:T(1024)S(1)}, u32[]{:S(2)}) copy-start(f32[768]{0:T(1024)S(1)} %get-tuple-element.964) | copy-start | bytes 9220 | tf_op jit(solution)/shard_map/while
  13.4 196.3 %copy-start.39 = (f32[768]{0:T(1024)}, f32[768]{0:T(1024)S(1)}, u32[]{:S(2)}) copy-start(f32[768]{0:T(1024)S(1)} %get-tuple-element.965) | copy-start | bytes 9220 | tf_op jit(solution)/shard_map/while
  24.9 42.4 %all-to-all-start = ((bf16[512,3,768]{0,1,2:T(4,128)(2,1)}), bf16[512,3,768]{0,1,2:T(4,128)(2,1)}, u32[]{:S(2)}, u32[]{:S(2)}) async-start(bf16[512,3,768]{0,1,2:T(4,128)(2,1)} %copy.93), calls=%async_computation | async-start | bytes 6291456 | tf_op jit(solution)/shard_map/while/body/eval_jaxpr/all_to_all | solution.py:165
  31.8 40.9 %copy-start.41 = (f32[3,192]{1,0:T(4,128)}, f32[3,192]{1,0:T(4,128)S(1)}, u32[]{:S(2)}) copy-start(f32[3,192]{1,0:T(4,128)S(1)} %get-tuple-element.830) | copy-start | bytes 6916 | tf_op jit(solution)/shard_map/while
  31.8 40.9 %copy-start.43 = (f32[3,192]{1,0:T(4,128)}, f32[3,192]{1,0:T(4,128)S(1)}, u32[]{:S(2)}) copy-start(f32[3,192]{1,0:T(4,128)S(1)} %get-tuple-element.828) | copy-start | bytes 6916 | tf_op jit(solution)/shard_map/while
  31.8 40.9 %copy-start.45 = (f32[3,192]{1,0:T(4,128)}, f32[3,192]{1,0:T(4,128)S(1)}, u32[]{:S(2)}) copy-start(f32[3,192]{1,0:T(4,128)S(1)} %get-tuple-element.829) | copy-start | bytes 6916 | tf_op jit(solution)/shard_map/while
  37.0 73.1 %copy-start.6 = (pred[512,2048]{1,0:T(8,128)(4,1)}, pred[512,2048]{1,0:T(8,128)(4,1)S(1)}, u32[]{:S(2)}) copy-start(pred[512,2048]{1,0:T(8,128)(4,1)S(1)} %get-tuple-element.837) | copy-start | bytes 3145732 | tf_op jit(solution)/shard_map/while
  37.0 92.6 %copy-start.9 = (pred[512,2048]{1,0:T(8,128)(4,1)}, pred[512,2048]{1,0:T(8,128)(4,1)S(1)}, u32[]{:S(2)}) copy-start(pred[512,2048]{1,0:T(8,128)(4,1)S(1)} %get-tuple-element.834) | copy-start | bytes 3145732 | tf_op jit(solution)/shard_map/while
  37.0 111.7 %copy-start.10 = (pred[512,2048]{1,0:T(8,128)(4,1)}, pred[512,2048]{1,0:T(8,128)(4,1)S(1)}, u32[]{:S(2)}) copy-start(pred[512,2048]{1,0:T(8,128)(4,1)S(1)} %get-tuple-element.831) | copy-start | bytes 3145732 | tf_op jit(solution)/shard_map/while
  78.1 70.6 %copy-start.2 = (bf16[2048,3,192]{0,2,1:T(8,128)(2,1)}, bf16[2048,3,192]{0,2,1:T(8,128)(2,1)S(1)}, u32[]{:S(2)}) copy-start(bf16[2048,3,192]{0,2,1:T(8,128)(2,1)S(1)} %add_convert_fusion.9) | copy-start | bytes 7077892 | tf_op jit(solution)/shard_map/while
  156.8 15.5 %all-to-all-start.1 = ((bf16[4,512,192]{1,2,0:T(8,128)(2,1)}), bf16[4,512,192]{1,2,0:T(8,128)(2,1)S(1)}, u32[]{:S(2)}, u32[]{:S(2)}) async-start(bf16[4,512,192]{1,2,0:T(8,128)(2,1)} %copy.96), calls=%async_computation.1 | async-start | bytes 1572864 | tf_op jit(solution)/shard_map/while/body/eval_jaxpr/all_to_all | solution.py:169
  192.8 22.5 %copy-start.18 = (f32[512,768]{1,0:T(8,128)}, f32[512,768]{1,0:T(8,128)S(1)}, u32[]{:S(2)}) copy-start(f32[512,768]{1,0:T(8,128)S(1)} %get-tuple-element.849) | copy-start | bytes 4718596 | tf_op jit(solution)/shard_map/while
  197.4 20.2 %all-to-all-start.2 = ((bf16[512,4,192]{0,2,1:T(8,128)(2,1)}), bf16[512,4,192]{0,2,1:T(8,128)(2,1)}, u32[]{:S(2)}, u32[]{:S(2)}) async-start(bf16[512,4,192]{0,2,1:T(8,128)(2,1)} %bitcast.484), calls=%async_computation.2 | async-start | bytes 1572864 | tf_op jit(solution)/shard_map/while/body/eval_jaxpr/all_to_all | solution.py:208
  219.6 19.5 %slice-start.6 = ((s8[12582912]{0:T(1024)(128)(4,1)}), s8[4194304]{0:T(1024)(128)(4,1)S(1)}, s32[]{:S(2)}) async-start(s8[12582912]{0:T(1024)(128)(4,1)} %bitcast.443), calls=%async_computation.18 | async-start | bytes 8388608 | tf_op jit(solution)/shard_map/while
  227.4 27.9 %slice-start = ((s8[12582912]{0:T(1024)(128)(4,1)}), s8[4194304]{0:T(1024)(128)(4,1)S(1)}, s32[]{:S(2)}) async-start(s8[12582912]{0:T(1024)(128)(4,1)} %bitcast.439), calls=%async_computation.12 | async-start | bytes 8388608 | tf_op jit(solution)/shard_map/while
  227.4 27.9 %slice-start.1 = ((s8[12582912]{0:T(1024)(128)(4,1)}), s8[4194304]{0:T(1024)(128)(4,1)S(1)}, s32[]{:S(2)}) async-start(s8[12582912]{0:T(1024)(128)(4,1)} %bitcast.439), calls=%async_computation.13 | async-start | bytes 8388608 | tf_op jit(solution)/shard_map/while
  364.8 53.4 %all-to-all-start.3 = ((bf16[2048,3,192]{2,1,0:T(4,128)(2,1)}), bf16[2048,3,192]{2,1,0:T(4,128)(2,1)}, u32[]{:S(2)}, u32[]{:S(2)}) async-start(bf16[2048,3,192]{2,1,0:T(4,128)(2,1)} %copy.98), calls=%async_computation.3 | async-start | bytes 8388608 | tf_op jit(solution)/shard_map/while/body/eval_jaxpr/all_to_all | solution.py:212
  392.5 33.1 %copy-start.48 = (f32[512]{0:T(512)S(1)}, f32[512]{0:T(512)}, u32[]{:S(2)}) copy-start(f32[512]{0:T(512)} %copy-done.47) | copy-start | bytes 6148 | tf_op jit(solution)/shard_map/while
  392.5 33.1 %copy-start.50 = (f32[512]{0:T(512)S(1)}, f32[512]{0:T(512)}, u32[]{:S(2)}) copy-start(f32[512]{0:T(512)} %copy-done.49) | copy-start | bytes 6148 | tf_op jit(solution)/shard_map/while
  392.6 38.7 %copy-start.52 = (f32[3,3,192]{2,1,0:T(4,128)}, f32[3,3,192]{2,1,0:T(4,128)S(1)}, u32[]{:S(2)}) copy-start(f32[3,3,192]{2,1,0:T(4,128)S(1)} %maximum_add_fusion.2) | copy-start | bytes 20740 | tf_op jit(solution)/shard_map/while
  439.8 187.8 %copy-start.72 = (f32[768]{0:T(1024)}, f32[768]{0:T(1024)S(1)}, u32[]{:S(2)}) copy-start(f32[768]{0:T(1024)S(1)} %get-tuple-element.969) | copy-start | bytes 9220 | tf_op jit(solution)/shard_map/while
  439.8 195.7 %copy-start.37 = (f32[768]{0:T(1024)}, f32[768]{0:T(1024)S(1)}, u32[]{:S(2)}) copy-start(f32[768]{0:T(1024)S(1)} %get-tuple-element.964) | copy-start | bytes 9220 | tf_op jit(solution)/shard_map/while
  439.8 195.7 %copy-start.39 = (f32[768]{0:T(1024)}, f32[768]{0:T(1024)S(1)}, u32[]{:S(2)}) copy-start(f32[768]{0:T(1024)S(1)} %get-tuple-element.965) | copy-start | bytes 9220 | tf_op jit(solution)/shard_map/while
  451.4 41.8 %all-to-all-start = ((bf16[512,3,768]{0,1,2:T(4,128)(2,1)}), bf16[512,3,768]{0,1,2:T(4,128)(2,1)}, u32[]{:S(2)}, u32[]{:S(2)}) async-start(bf16[512,3,768]{0,1,2:T(4,128)(2,1)} %copy.93), calls=%async_computation | async-start | bytes 6291456 | tf_op jit(solution)/shard_map/while/body/eval_jaxpr/all_to_all | solution.py:165
  458.3 40.3 %copy-start.41 = (f32[3,192]{1,0:T(4,128)}, f32[3,192]{1,0:T(4,128)S(1)}, u32[]{:S(2)}) copy-start(f32[3,192]{1,0:T(4,128)S(1)} %get-tuple-element.830) | copy-start | bytes 6916 | tf_op jit(solution)/shard_map/while
  458.3 40.3 %copy-start.43 = (f32[3,192]{1,0:T(4,128)}, f32[3,192]{1,0:T(4,128)S(1)}, u32[]{:S(2)}) copy-start(f32[3,192]{1,0:T(4,128)S(1)} %get-tuple-element.828) | copy-start | bytes 6916 | tf_op jit(solution)/shard_map/while
  458.3 40.3 %copy-start.45 = (f32[3,192]{1,0:T(4,128)}, f32[3,192]{1,0:T(4,128)S(1)}, u32[]{:S(2)}) copy-start(f32[3,192]{1,0:T(4,128)S(1)} %get-tuple-element.829) | copy-start | bytes 6916 | tf_op jit(solution)/shard_map/while
  463.4 72.5 %copy-start.6 = (pred[512,2048]{1,0:T(8,128)(4,1)}, pred[512,2048]{1,0:T(8,128)(4,1)S(1)}, u32[]{:S(2)}) copy-start(pred[512,2048]{1,0:T(8,128)(4,1)S(1)} %get-tuple-element.837) | copy-start | bytes 3145732 | tf_op jit(solution)/shard_map/while
  463.4 91.9 %copy-start.9 = (pred[512,2048]{1,0:T(8,128)(4,1)}, pred[512,2048]{1,0:T(8,128)(4,1)S(1)}, u32[]{:S(2)}) copy-start(pred[512,2048]{1,0:T(8,128)(4,1)S(1)} %get-tuple-element.834) | copy-start | bytes 3145732 | tf_op jit(solution)/shard_map/while
  463.4 111.1 %copy-start.10 = (pred[512,2048]{1,0:T(8,128)(4,1)}, pred[512,2048]{1,0:T(8,128)(4,1)S(1)}, u32[]{:S(2)}) copy-start(pred[512,2048]{1,0:T(8,128)(4,1)S(1)} %get-tuple-element.831) | copy-start | bytes 3145732 | tf_op jit(solution)/shard_map/while
  503.9 70.6 %copy-start.2 = (bf16[2048,3,192]{0,2,1:T(8,128)(2,1)}, bf16[2048,3,192]{0,2,1:T(8,128)(2,1)S(1)}, u32[]{:S(2)}) copy-start(bf16[2048,3,192]{0,2,1:T(8,128)(2,1)S(1)} %add_convert_fusion.9) | copy-start | bytes 7077892 | tf_op jit(solution)/shard_map/while
  581.0 18.1 %copy-start.22 = (bf16[2,512,768]{2,1,0:T(8,128)(2,1)S(1)}, bf16[2,512,768]{2,1,0:T(8,128)(2,1)}, u32[]{:S(2)}) copy-start(bf16[2,512,768]{2,1,0:T(8,128)(2,1)} %get-tuple-element.957) | copy-start | bytes 4718596 | tf_op jit(solution)/shard_map/while
  582.7 15.5 %all-to-all-start.1 = ((bf16[4,512,192]{1,2,0:T(8,128)(2,1)}), bf16[4,512,192]{1,2,0:T(8,128)(2,1)S(1)}, u32[]{:S(2)}, u32[]{:S(2)}) async-start(bf16[4,512,192]{1,2,0:T(8,128)(2,1)} %copy.96), calls=%async_computation.1 | async-start | bytes 1572864 | tf_op jit(solution)/shard_map/while/body/eval_jaxpr/all_to_all | solution.py:169
  618.7 24.9 %copy-start.18 = (f32[512,768]{1,0:T(8,128)}, f32[512,768]{1,0:T(8,128)S(1)}, u32[]{:S(2)}) copy-start(f32[512,768]{1,0:T(8,128)S(1)} %get-tuple-element.849) | copy-start | bytes 4718596 | tf_op jit(solution)/shard_map/while
  623.3 24.3 %all-to-all-start.2 = ((bf16[512,4,192]{0,2,1:T(8,128)(2,1)}), bf16[512,4,192]{0,2,1:T(8,128)(2,1)}, u32[]{:S(2)}, u32[]{:S(2)}) async-start(bf16[512,4,192]{0,2,1:T(8,128)(2,1)} %bitcast.484), calls=%async_computation.2 | async-start | bytes 1572864 | tf_op jit(solution)/shard_map/while/body/eval_jaxpr/all_to_all | solution.py:208
  649.5 19.5 %slice-start.6 = ((s8[12582912]{0:T(1024)(128)(4,1)}), s8[4194304]{0:T(1024)(128)(4,1)S(1)}, s32[]{:S(2)}) async-start(s8[12582912]{0:T(1024)(128)(4,1)} %bitcast.443), calls=%async_computation.18 | async-start | bytes 8388608 | tf_op jit(solution)/shard_map/while
  657.4 27.9 %slice-start = ((s8[12582912]{0:T(1024)(128)(4,1)}), s8[4194304]{0:T(1024)(128)(4,1)S(1)}, s32[]{:S(2)}) async-start(s8[12582912]{0:T(1024)(128)(4,1)} %bitcast.439), calls=%async_computation.12 | async-start | bytes 8388608 | tf_op jit(solution)/shard_map/while
  657.4 27.9 %slice-start.1 = ((s8[12582912]{0:T(1024)(128)(4,1)}), s8[4194304]{0:T(1024)(128)(4,1)S(1)}, s32[]{:S(2)}) async-start(s8[12582912]{0:T(1024)(128)(4,1)} %bitcast.439), calls=%async_computation.13 | async-start | bytes 8388608 | tf_op jit(solution)/shard_map/while
  794.8 53.4 %all-to-all-start.3 = ((bf16[2048,3,192]{2,1,0:T(4,128)(2,1)}), bf16[2048,3,192]{2,1,0:T(4,128)(2,1)}, u32[]{:S(2)}, u32[]{:S(2)}) async-start(bf16[2048,3,192]{2,1,0:T(4,128)(2,1)} %copy.98), calls=%async_computation.3 | async-start | bytes 8388608 | tf_op jit(solution)/shard_map/while/body/eval_jaxpr/all_to_all | solution.py:212
  825.2 30.4 %copy-start.48 = (f32[512]{0:T(512)S(1)}, f32[512]{0:T(512)}, u32[]{:S(2)}) copy-start(f32[512]{0:T(512)} %copy-done.47) | copy-start | bytes 6148 | tf_op jit(solution)/shard_map/while
  825.2 30.4 %copy-start.50 = (f32[512]{0:T(512)S(1)}, f32[512]{0:T(512)}, u32[]{:S(2)}) copy-start(f32[512]{0:T(512)} %copy-done.49) | copy-start | bytes 6148 | tf_op jit(solution)/shard_map/while
  825.3 36.0 %copy-start.52 = (f32[3,3,192]{2,1,0:T(4,128)}, f32[3,3,192]{2,1,0:T(4,128)S(1)}, u32[]{:S(2)}) copy-start(f32[3,3,192]{2,1,0:T(4,128)S(1)} %maximum_add_fusion.2) | copy-start | bytes 20740 | tf_op jit(solution)/shard_map/while
  872.8 242.3 %reduce-scatter.6.cloned.1.call-start = ((), (), s32[]{:S(2)}) async-start(), calls=%async_computation.8 | async-start | bytes 9732096 | tf_op jit(solution)/shard_map/reduce_scatter | solution.py:265
  893.5 362.8 %reduce-scatter.10.cloned.1.call-start = ((), (), s32[]{:S(2)}) async-start(), calls=%async_computation.10 | async-start | bytes 9732096 | tf_op jit(solution)/shard_map/reduce_scatter | solution.py:270
  894.2 504.0 %reduce-scatter.12.cloned.1.call-start = ((), (), s32[]{:S(2)}) async-start(), calls=%async_computation.11 | async-start | bytes 9732096 | tf_op jit(solution)/shard_map/reduce_scatter | solution.py:272
  894.3 504.0 %copy-start.1 = (bf16[3,3,768]{2,1,0:T(4,128)(2,1)S(1)}, bf16[3,3,768]{2,1,0:T(4,128)(2,1)}, u32[]{:S(2)}) copy-start(bf16[3,3,768]{2,1,0:T(4,128)(2,1)} %param.22) | copy-start | bytes 41476
  (146 other events, 803.7 us)
Sparse Core Ops, SparseCore 0:
  872.9 100.1 reduce-scatter.7
  980.6 134.4 reduce-scatter.5
  1121.6 134.6 reduce-scatter.9
  1263.6 134.5 reduce-scatter.11
where the time goes:
time: 1410 us
  waiting for transfers between devices  589 us (42%)
  matrix products  409 us (29%)
  other arithmetic  180 us (13%)
  local copies, waits for them, and re-layouts  127 us (9%)
  blocking collectives  41.7 us (3%)
  starting transfers between devices  36.8 us (3%)
  between operations  14.4 us (1%)
    reduce_scatter x1, waiting for transfers between devices, on_device(): lax.psum_scatter(qkv_flat, ('batch', 'mp'), scatter_dimension=0, tiled=True)  142 us
    reduce_scatter x1, waiting for transfers between devices, on_device(): lax.psum_scatter(running[9], ('batch', 'mp'), scatter_dimension=0, tiled=...  142 us
    reduce_scatter x1, waiting for transfers between devices, on_device(): lax.psum_scatter(running[7], ('batch', 'mp'), scatter_dimension=0, tiled=...  141 us
    dot_general x8, matrix products, attend_backward(): jnp.einsum('qhd,khd->hqk', block_grad, values, preferred_element_type=jnp...  80.2 us
    convert_element_type x8, other arithmetic, attend_backward(): grad_scores = (prob_block * (grad_probs - row_delta)).astype(jnp.bfloat16)  71.2 us
    all_to_all x2, waiting for transfers between devices, one_batch(): lax.all_to_all(local_proj, 'mp', split_axis=2, concat_axis=0, tiled=True)  60.2 us
    dot_general x8, matrix products, attend_backward(): jnp.einsum('hqk,qhd->khd', prob_block.astype(jnp.bfloat16), block_grad, p...  59.4 us
    reduce_sum x8, other arithmetic, attend_forward(): log_total = jax.nn.logsumexp(scores, axis=-1, keepdims=True)  54.1 us
  transfers between devices with their start and end apart: 12, of which 10 were waited for; matrix products, arithmetic and copies ran while one was open for 9% of the time, Pallas kernels for 0%

commit v1 on v0

--- a/solution.py
+++ b/solution.py
@@ -7,6 +7,13 @@
 QBLOCK = 512
 EPSILON = 1e-05
 NEGATIVE = -1000000000.0
+
+
+def stacked_exchange(block, name, split, join):
+    size = lax.axis_size(name)
+    blocks = jnp.stack(jnp.split(block, size, axis=split), axis=0)
+    blocks = lax.all_to_all(blocks, name, split_axis=0, concat_axis=0)
+    return jnp.concatenate(blocks, axis=join)
 
 
 def norm_forward(values, norm_gain, offset):
@@ -209,7 +216,7 @@
         grad_mixed = attend_backward(mixed_b, grad_heads, log_totals, length)
         grad_proj, grad_conv = conv_backward(grad_mixed, kernel_own, padded)
         grad_proj_b = grad_proj.astype(jnp.bfloat16)
-        grad_proj_tok = lax.all_to_all(grad_proj_b, "mp", split_axis=0, concat_axis=2, tiled=True)
+        grad_proj_tok = stacked_exchange(grad_proj_b, "mp", 0, 2)
         grad_qkv = jnp.einsum(
             "td,tce->cde", normed_b, grad_proj_tok, preferred_element_type=jnp.float32
         )

time: 1410 us -> 1340 us (0.950)
  waiting for transfers between devices: 589 us -> 550 us
  local copies, waits for them, and re-layouts: 127 us -> 100 us
    all_to_all x2, waiting for transfers between devices: 48.6 us -> 8.67 us  [stacked_exchange(): blocks = lax.all_to_all(blocks, name, split_axis=0, concat_axis=0)]
    all_to_all x2 -> x0, local copies, waits for them, and re-layouts: 14.7 us -> none  [one_batch(): lax.all_to_all(grad_proj_b, 'mp', split_axis=0, concat_axis=2, tiled=True)]
where the time goes in v1:
time: 1340 us
  waiting for transfers between devices  550 us (41%)
  matrix products  411 us (31%)
  other arithmetic  178 us (13%)
  local copies, waits for them, and re-layouts  100 us (7%)
  blocking collectives  41.7 us (3%)
  starting transfers between devices  35.8 us (3%)
  between operations  14.4 us (1%)
    reduce_scatter x1, waiting for transfers between devices, on_device(): lax.psum_scatter(qkv_flat, ('batch', 'mp'), scatter_dimension=0, tiled=True)  142 us
    reduce_scatter x1, waiting for transfers between devices, on_device(): lax.psum_scatter(running[9], ('batch', 'mp'), scatter_dimension=0, tiled=...  142 us
    reduce_scatter x1, waiting for transfers between devices, on_device(): lax.psum_scatter(running[7], ('batch', 'mp'), scatter_dimension=0, tiled=...  141 us
    dot_general x8, matrix products, attend_backward(): jnp.einsum('qhd,khd->hqk', block_grad, values, preferred_element_type=jnp...  80.2 us
    convert_element_type x8, other arithmetic, attend_backward(): grad_scores = (prob_block * (grad_probs - row_delta)).astype(jnp.bfloat16)  71.2 us
    all_to_all x2, waiting for transfers between devices, one_batch(): lax.all_to_all(local_proj, 'mp', split_axis=2, concat_axis=0, tiled=True)  61.6 us
    dot_general x8, matrix products, attend_backward(): jnp.einsum('hqk,qhd->khd', prob_block.astype(jnp.bfloat16), block_grad, p...  59.4 us
    reduce_sum x8, other arithmetic, attend_forward(): log_total = jax.nn.logsumexp(scores, axis=-1, keepdims=True)  54.1 us
  transfers between devices with their start and end apart: 12, of which 10 were waited for; matrix products, arithmetic and copies ran while one was open for 9% of the time, Pallas kernels for 0%

profile of v1, /device:TPU:0, one launch (start us, length us, event | category | flops | bytes accessed | tf_op | source)
XLA Modules:
  0.0 1338.9 jit_solution(11107977282937041646)
XLA Ops:
  11.6 794.9 %while.37 = (s32[]{:T(128)}, f32[768]{0:T(1024)}, f32[768]{0:T(1024)}, f32[3,768,768]{1,2,0:T(8,128)}, f32[3,3,192]{2,1,0:T(4,128)}, /*index=5*/f32[768,768]{1,0...) while((s32[]{:T(128)}, f32[768]{0:T(1024)}, ...), condition=%wide.region_30.31_spmd.clone, body=%wide.region_0.30_spmd.clone.sunk | while | flops 31856164864 | bytes 1239124352 | solution.py:258
  34.5 31.1 %all-to-all-done = bf16[512,3,768]{0,1,2:T(4,128)(2,1)} async-done(((bf16[512,3,768]{0,1,2:T(4,128)(2,1)}), bf16[512,3,768]{0,1,2:T(4,128)(2,1)}, u32[]{:S(2)}, u32[]{:S(2)}) %all-to-all-start) | async-done | bytes 2359328 | tf_op jit(solution)/shard_map/while/body/eval_jaxpr/all_to_all | solution.py:172
  101.2 6.8 exponential_reduce_fusion.10
  120.5 6.8 exponential_reduce_fusion.9
  139.5 6.8 exponential_reduce_fusion.8
  159.1 10.9 all-to-all-done.1
  178.6 7.7 convert_reduce_fusion.7
  199.5 7.8 fusion.265
  217.3 7.8 fusion.255
  225.1 11.6 multiply_reduce_fusion.19
  236.8 8.8 multiply_convert_fusion.16
  253.0 8.9 multiply_reduce_fusion.20
  261.9 6.9 convolution_add_fusion.11
  268.8 9.3 multiply_reduce_fusion.21
  284.7 10.3 multiply_reduce_fusion.22
  295.0 8.4 convolution_add_fusion.13
  303.4 9.8 multiply_convert_fusion.19
  316.0 9.9 multiply_convert_fusion.18
  331.6 7.0 multiply_convert_fusion.17
  361.2 9.5 select_add_fusion.22
  427.6 30.5 %all-to-all-done = bf16[512,3,768]{0,1,2:T(4,128)(2,1)} async-done(((bf16[512,3,768]{0,1,2:T(4,128)(2,1)}), bf16[512,3,768]{0,1,2:T(4,128)(2,1)}, u32[]{:S(2)}, u32[]{:S(2)}) %all-to-all-start) | async-done | bytes 2359328 | tf_op jit(solution)/shard_map/while/body/eval_jaxpr/all_to_all | solution.py:172
  493.6 6.8 exponential_reduce_fusion.10
  512.9 6.8 exponential_reduce_fusion.9
  532.0 6.8 exponential_reduce_fusion.8
  551.5 10.9 all-to-all-done.1
  571.0 7.7 convert_reduce_fusion.7
  592.0 7.8 fusion.265
  599.8 8.0 select_add_fusion.20
  613.8 7.8 fusion.255
  621.7 11.6 multiply_reduce_fusion.19
  633.3 8.8 multiply_convert_fusion.16
  649.6 8.9 multiply_reduce_fusion.20
  658.5 6.9 convolution_add_fusion.11
  665.3 9.3 multiply_reduce_fusion.21
  681.2 10.3 multiply_reduce_fusion.22
  691.6 8.4 convolution_add_fusion.13
  700.0 9.8 multiply_convert_fusion.19
  712.6 9.9 multiply_convert_fusion.18
  728.2 7.0 multiply_convert_fusion.17
  757.8 12.3 select_add_fusion.22
  792.8 8.3 bitcast_add_fusion.2
  806.6 10.4 reshape.467
  817.0 10.1 copy.60
  828.9 41.7 %all-reduce.9 = (f32[768]{0:T(1024)S(1)}, f32[768]{0:T(1024)S(1)}, f32[3,3,768]{2,1,0:T(4,128)S(1)}, f32[768]{0:T(1024)S(1)}, f32[768]{0:T(1024)S(1)}, /*index=5*/f32[3072]{0:T(1024)S(1)}, f32[768]{0:T(1024)S(1)}) all-reduce(f32[768]{0:T(1024)S(1)} %copy-done.74, ...), channel_id=2, replica_groups=mesh['batch'=8,'mp'=4] {'batch','mp'}, use_global_device_ids=true, to_apply=%region_31.32.clone | all-reduce | flops 13824 | bytes 110592
  874.8 32.0 %reduce-scatter.8.cloned.1.call-done = f32[24,768]{1,0:T(8,128)} async-done(((f32[768,768]{1,0:T(8,128)}), f32[24,768]{1,0:T(8,128)}) %reduce-scatter.8.cloned.1.call-update) | async-done | bytes 73744 | tf_op jit(solution)/shard_map/reduce_scatter | solution.py:274
  906.8 142.2 %reduce-scatter.6.cloned.1.call-done = f32[288,192]{1,0:T(8,128)} async-done(((f32[9216,192]{1,0:T(8,128)}), f32[288,192]{1,0:T(8,128)}) %reduce-scatter.6.cloned.1.call-update) | async-done | bytes 221200 | tf_op jit(solution)/shard_map/reduce_scatter | solution.py:272
  1049.0 141.1 %reduce-scatter.10.cloned.1.call-done = f32[24,3072]{1,0:T(8,128)} async-done(((f32[768,3072]{1,0:T(8,128)}), f32[24,3072]{1,0:T(8,128)}) %reduce-scatter.10.cloned.1.call-update) | async-done | bytes 294928 | tf_op jit(solution)/shard_map/reduce_scatter | solution.py:277
  1190.1 141.9 %reduce-scatter.12.cloned.1.call-done = f32[96,768]{1,0:T(8,128)} async-done(((f32[3072,768]{1,0:T(8,128)}), f32[96,768]{1,0:T(8,128)}) %reduce-scatter.12.cloned.1.call-update) | async-done | bytes 294928 | tf_op jit(solution)/shard_map/reduce_scatter | solution.py:279
  (604 shorter events, 407.5 us)
Async XLA Ops:
  7.2 899.6 %reduce-scatter.8.cloned.1.call-start = ((), (), s32[]{:S(2)}) async-start(), calls=%async_computation.9 | async-start | bytes 2433024 | tf_op jit(solution)/shard_map/reduce_scatter | solution.py:274
  11.6 17.7 %copy-start.51 = (f32[3,3,192]{2,0,1:T(4,128)}, f32[3,3,192]{2,0,1:T(4,128)S(1)}, u32[]{:S(2)}) copy-start(f32[3,3,192]{2,0,1:T(4,128)S(1)} %get-tuple-element.968) | copy-start | bytes 20740 | tf_op jit(solution)/shard_map/while
  11.6 187.9 %copy-start.76 = (f32[768]{0:T(1024)}, f32[768]{0:T(1024)S(1)}, u32[]{:S(2)}) copy-start(f32[768]{0:T(1024)S(1)} %get-tuple-element.981) | copy-start | bytes 9220 | tf_op jit(solution)/shard_map/while
  11.6 195.8 %copy-start.35 = (f32[768]{0:T(1024)}, f32[768]{0:T(1024)S(1)}, u32[]{:S(2)}) copy-start(f32[768]{0:T(1024)S(1)} %get-tuple-element.976) | copy-start | bytes 9220 | tf_op jit(solution)/shard_map/while
  11.6 195.7 %copy-start.37 = (f32[768]{0:T(1024)}, f32[768]{0:T(1024)S(1)}, u32[]{:S(2)}) copy-start(f32[768]{0:T(1024)S(1)} %get-tuple-element.977) | copy-start | bytes 9220 | tf_op jit(solution)/shard_map/while
  23.2 42.4 %all-to-all-start = ((bf16[512,3,768]{0,1,2:T(4,128)(2,1)}), bf16[512,3,768]{0,1,2:T(4,128)(2,1)}, u32[]{:S(2)}, u32[]{:S(2)}) async-start(bf16[512,3,768]{0,1,2:T(4,128)(2,1)} %copy.76), calls=%async_computation | async-start | bytes 6291456 | tf_op jit(solution)/shard_map/while/body/eval_jaxpr/all_to_all | solution.py:172
  29.3 41.6 %copy-start.39 = (f32[3,192]{1,0:T(4,128)}, f32[3,192]{1,0:T(4,128)S(1)}, u32[]{:S(2)}) copy-start(f32[3,192]{1,0:T(4,128)S(1)} %get-tuple-element.838) | copy-start | bytes 6916 | tf_op jit(solution)/shard_map/while
  29.3 41.6 %copy-start.41 = (f32[3,192]{1,0:T(4,128)}, f32[3,192]{1,0:T(4,128)S(1)}, u32[]{:S(2)}) copy-start(f32[3,192]{1,0:T(4,128)S(1)} %get-tuple-element.836) | copy-start | bytes 6916 | tf_op jit(solution)/shard_map/while
  29.3 41.6 %copy-start.43 = (f32[3,192]{1,0:T(4,128)}, f32[3,192]{1,0:T(4,128)S(1)}, u32[]{:S(2)}) copy-start(f32[3,192]{1,0:T(4,128)S(1)} %get-tuple-element.837) | copy-start | bytes 6916 | tf_op jit(solution)/shard_map/while
  34.5 73.4 %copy-start.6 = (pred[512,2048]{1,0:T(8,128)(4,1)}, pred[512,2048]{1,0:T(8,128)(4,1)S(1)}, u32[]{:S(2)}) copy-start(pred[512,2048]{1,0:T(8,128)(4,1)S(1)} %get-tuple-element.845) | copy-start | bytes 3145732 | tf_op jit(solution)/shard_map/while
  34.5 92.7 %copy-start.9 = (pred[512,2048]{1,0:T(8,128)(4,1)}, pred[512,2048]{1,0:T(8,128)(4,1)S(1)}, u32[]{:S(2)}) copy-start(pred[512,2048]{1,0:T(8,128)(4,1)S(1)} %get-tuple-element.842) | copy-start | bytes 3145732 | tf_op jit(solution)/shard_map/while
  34.5 111.8 %copy-start.10 = (pred[512,2048]{1,0:T(8,128)(4,1)}, pred[512,2048]{1,0:T(8,128)(4,1)S(1)}, u32[]{:S(2)}) copy-start(pred[512,2048]{1,0:T(8,128)(4,1)S(1)} %get-tuple-element.839) | copy-start | bytes 3145732 | tf_op jit(solution)/shard_map/while
  76.3 70.0 %copy-start.2 = (bf16[2048,3,192]{0,2,1:T(8,128)(2,1)}, bf16[2048,3,192]{0,2,1:T(8,128)(2,1)S(1)}, u32[]{:S(2)}) copy-start(bf16[2048,3,192]{0,2,1:T(8,128)(2,1)S(1)} %add_convert_fusion.9) | copy-start | bytes 7077892 | tf_op jit(solution)/shard_map/while
  152.8 18.1 %copy-start.20 = (bf16[2,512,768]{2,1,0:T(8,128)(2,1)S(1)}, bf16[2,512,768]{2,1,0:T(8,128)(2,1)}, u32[]{:S(2)}) copy-start(bf16[2,512,768]{2,1,0:T(8,128)(2,1)} %get-tuple-element.969) | copy-start | bytes 4718596 | tf_op jit(solution)/shard_map/while
  154.5 15.5 %all-to-all-start.1 = ((bf16[4,512,192]{1,2,0:T(8,128)(2,1)}), bf16[4,512,192]{1,2,0:T(8,128)(2,1)S(1)}, u32[]{:S(2)}, u32[]{:S(2)}) async-start(bf16[4,512,192]{1,2,0:T(8,128)(2,1)} %copy.79), calls=%async_computation.1 | async-start | bytes 1572864 | tf_op jit(solution)/shard_map/while/body/eval_jaxpr/all_to_all | solution.py:176
  190.5 22.5 %copy-start.18 = (f32[512,768]{1,0:T(8,128)}, f32[512,768]{1,0:T(8,128)S(1)}, u32[]{:S(2)}) copy-start(f32[512,768]{1,0:T(8,128)S(1)} %get-tuple-element.857) | copy-start | bytes 4718596 | tf_op jit(solution)/shard_map/while
  195.1 20.2 %all-to-all-start.2 = ((bf16[512,4,192]{0,2,1:T(8,128)(2,1)}), bf16[512,4,192]{0,2,1:T(8,128)(2,1)}, u32[]{:S(2)}, u32[]{:S(2)}) async-start(bf16[512,4,192]{0,2,1:T(8,128)(2,1)} %bitcast.489), calls=%async_computation.2 | async-start | bytes 1572864 | tf_op jit(solution)/shard_map/while/body/eval_jaxpr/all_to_all | solution.py:215
  217.3 19.5 %slice-start.6 = ((s8[12582912]{0:T(1024)(128)(4,1)}), s8[4194304]{0:T(1024)(128)(4,1)S(1)}, s32[]{:S(2)}) async-start(s8[12582912]{0:T(1024)(128)(4,1)} %bitcast.450), calls=%async_computation.18 | async-start | bytes 8388608 | tf_op jit(solution)/shard_map/while
  225.1 27.9 %slice-start = ((s8[12582912]{0:T(1024)(128)(4,1)}), s8[4194304]{0:T(1024)(128)(4,1)S(1)}, s32[]{:S(2)}) async-start(s8[12582912]{0:T(1024)(128)(4,1)} %bitcast.446), calls=%async_computation.12 | async-start | bytes 8388608 | tf_op jit(solution)/shard_map/while
  225.1 27.9 %slice-start.1 = ((s8[12582912]{0:T(1024)(128)(4,1)}), s8[4194304]{0:T(1024)(128)(4,1)S(1)}, s32[]{:S(2)}) async-start(s8[12582912]{0:T(1024)(128)(4,1)} %bitcast.446), calls=%async_computation.13 | async-start | bytes 8388608 | tf_op jit(solution)/shard_map/while
  236.8 16.2 %slice-start.2 = ((s8[12582912]{0:T(1024)(128)(4,1)}), s8[4194304]{0:T(1024)(128)(4,1)S(1)}, s32[]{:S(2)}) async-start(s8[12582912]{0:T(1024)(128)(4,1)} %bitcast.446), calls=%async_computation.14 | async-start | bytes 8388608 | tf_op jit(solution)/shard_map/while
  253.0 15.8 %slice-start.3 = ((s8[12582912]{0:T(1024)(128)(4,1)}), s8[4194304]{0:T(1024)(128)(4,1)S(1)}, s32[]{:S(2)}) async-start(s8[12582912]{0:T(1024)(128)(4,1)} %bitcast.448), calls=%async_computation.15 | async-start | bytes 8388608 | tf_op jit(solution)/shard_map/while
  356.4 33.3 %all-to-all-start.3 = ((bf16[4,512,3,192]{1,3,2,0:T(8,128)(2,1)}), bf16[4,512,3,192]{1,3,2,0:T(8,128)(2,1)}, u32[]{:S(2)}, u32[]{:S(2)}) async-start(bf16[4,512,3,192]{1,3,2,0:T(8,128)(2,1)} %pad_maximum_fusion.9), calls=%async_computation.3 | async-start | bytes 4718592 | tf_op jit(solution)/shard_map/while/body/eval_jaxpr/all_to_all | solution.py:15
  404.7 17.7 %copy-start.51 = (f32[3,3,192]{2,0,1:T(4,128)}, f32[3,3,192]{2,0,1:T(4,128)S(1)}, u32[]{:S(2)}) copy-start(f32[3,3,192]{2,0,1:T(4,128)S(1)} %get-tuple-element.968) | copy-start | bytes 20740 | tf_op jit(solution)/shard_map/while
  404.7 187.3 %copy-start.76 = (f32[768]{0:T(1024)}, f32[768]{0:T(1024)S(1)}, u32[]{:S(2)}) copy-start(f32[768]{0:T(1024)S(1)} %get-tuple-element.981) | copy-start | bytes 9220 | tf_op jit(solution)/shard_map/while
  404.7 195.1 %copy-start.35 = (f32[768]{0:T(1024)}, f32[768]{0:T(1024)S(1)}, u32[]{:S(2)}) copy-start(f32[768]{0:T(1024)S(1)} %get-tuple-element.976) | copy-start | bytes 9220 | tf_op jit(solution)/shard_map/while
  404.7 195.1 %copy-start.37 = (f32[768]{0:T(1024)}, f32[768]{0:T(1024)S(1)}, u32[]{:S(2)}) copy-start(f32[768]{0:T(1024)S(1)} %get-tuple-element.977) | copy-start | bytes 9220 | tf_op jit(solution)/shard_map/while
  416.3 41.8 %all-to-all-start = ((bf16[512,3,768]{0,1,2:T(4,128)(2,1)}), bf16[512,3,768]{0,1,2:T(4,128)(2,1)}, u32[]{:S(2)}, u32[]{:S(2)}) async-start(bf16[512,3,768]{0,1,2:T(4,128)(2,1)} %copy.76), calls=%async_computation | async-start | bytes 6291456 | tf_op jit(solution)/shard_map/while/body/eval_jaxpr/all_to_all | solution.py:172
  422.4 41.0 %copy-start.39 = (f32[3,192]{1,0:T(4,128)}, f32[3,192]{1,0:T(4,128)S(1)}, u32[]{:S(2)}) copy-start(f32[3,192]{1,0:T(4,128)S(1)} %get-tuple-element.838) | copy-start | bytes 6916 | tf_op jit(solution)/shard_map/while
  422.4 41.0 %copy-start.41 = (f32[3,192]{1,0:T(4,128)}, f32[3,192]{1,0:T(4,128)S(1)}, u32[]{:S(2)}) copy-start(f32[3,192]{1,0:T(4,128)S(1)} %get-tuple-element.836) | copy-start | bytes 6916 | tf_op jit(solution)/shard_map/while
  422.4 41.0 %copy-start.43 = (f32[3,192]{1,0:T(4,128)}, f32[3,192]{1,0:T(4,128)S(1)}, u32[]{:S(2)}) copy-start(f32[3,192]{1,0:T(4,128)S(1)} %get-tuple-element.837) | copy-start | bytes 6916 | tf_op jit(solution)/shard_map/while
  427.6 72.8 %copy-start.6 = (pred[512,2048]{1,0:T(8,128)(4,1)}, pred[512,2048]{1,0:T(8,128)(4,1)S(1)}, u32[]{:S(2)}) copy-start(pred[512,2048]{1,0:T(8,128)(4,1)S(1)} %get-tuple-element.845) | copy-start | bytes 3145732 | tf_op jit(solution)/shard_map/while
  427.6 92.1 %copy-start.9 = (pred[512,2048]{1,0:T(8,128)(4,1)}, pred[512,2048]{1,0:T(8,128)(4,1)S(1)}, u32[]{:S(2)}) copy-start(pred[512,2048]{1,0:T(8,128)(4,1)S(1)} %get-tuple-element.842) | copy-start | bytes 3145732 | tf_op jit(solution)/shard_map/while
  427.6 111.2 %copy-start.10 = (pred[512,2048]{1,0:T(8,128)(4,1)}, pred[512,2048]{1,0:T(8,128)(4,1)S(1)}, u32[]{:S(2)}) copy-start(pred[512,2048]{1,0:T(8,128)(4,1)S(1)} %get-tuple-element.839) | copy-start | bytes 3145732 | tf_op jit(solution)/shard_map/while
  468.7 70.0 %copy-start.2 = (bf16[2048,3,192]{0,2,1:T(8,128)(2,1)}, bf16[2048,3,192]{0,2,1:T(8,128)(2,1)S(1)}, u32[]{:S(2)}) copy-start(bf16[2048,3,192]{0,2,1:T(8,128)(2,1)S(1)} %add_convert_fusion.9) | copy-start | bytes 7077892 | tf_op jit(solution)/shard_map/while
  545.2 18.1 %copy-start.20 = (bf16[2,512,768]{2,1,0:T(8,128)(2,1)S(1)}, bf16[2,512,768]{2,1,0:T(8,128)(2,1)}, u32[]{:S(2)}) copy-start(bf16[2,512,768]{2,1,0:T(8,128)(2,1)} %get-tuple-element.969) | copy-start | bytes 4718596 | tf_op jit(solution)/shard_map/while
  547.0 15.5 %all-to-all-start.1 = ((bf16[4,512,192]{1,2,0:T(8,128)(2,1)}), bf16[4,512,192]{1,2,0:T(8,128)(2,1)S(1)}, u32[]{:S(2)}, u32[]{:S(2)}) async-start(bf16[4,512,192]{1,2,0:T(8,128)(2,1)} %copy.79), calls=%async_computation.1 | async-start | bytes 1572864 | tf_op jit(solution)/shard_map/while/body/eval_jaxpr/all_to_all | solution.py:176
  583.0 24.9 %copy-start.18 = (f32[512,768]{1,0:T(8,128)}, f32[512,768]{1,0:T(8,128)S(1)}, u32[]{:S(2)}) copy-start(f32[512,768]{1,0:T(8,128)S(1)} %get-tuple-element.857) | copy-start | bytes 4718596 | tf_op jit(solution)/shard_map/while
  587.6 24.3 %all-to-all-start.2 = ((bf16[512,4,192]{0,2,1:T(8,128)(2,1)}), bf16[512,4,192]{0,2,1:T(8,128)(2,1)}, u32[]{:S(2)}, u32[]{:S(2)}) async-start(bf16[512,4,192]{0,2,1:T(8,128)(2,1)} %bitcast.489), calls=%async_computation.2 | async-start | bytes 1572864 | tf_op jit(solution)/shard_map/while/body/eval_jaxpr/all_to_all | solution.py:215
  613.8 19.5 %slice-start.6 = ((s8[12582912]{0:T(1024)(128)(4,1)}), s8[4194304]{0:T(1024)(128)(4,1)S(1)}, s32[]{:S(2)}) async-start(s8[12582912]{0:T(1024)(128)(4,1)} %bitcast.450), calls=%async_computation.18 | async-start | bytes 8388608 | tf_op jit(solution)/shard_map/while
  621.7 27.9 %slice-start = ((s8[12582912]{0:T(1024)(128)(4,1)}), s8[4194304]{0:T(1024)(128)(4,1)S(1)}, s32[]{:S(2)}) async-start(s8[12582912]{0:T(1024)(128)(4,1)} %bitcast.446), calls=%async_computation.12 | async-start | bytes 8388608 | tf_op jit(solution)/shard_map/while
  621.7 27.9 %slice-start.1 = ((s8[12582912]{0:T(1024)(128)(4,1)}), s8[4194304]{0:T(1024)(128)(4,1)S(1)}, s32[]{:S(2)}) async-start(s8[12582912]{0:T(1024)(128)(4,1)} %bitcast.446), calls=%async_computation.13 | async-start | bytes 8388608 | tf_op jit(solution)/shard_map/while
  633.3 16.2 %slice-start.2 = ((s8[12582912]{0:T(1024)(128)(4,1)}), s8[4194304]{0:T(1024)(128)(4,1)S(1)}, s32[]{:S(2)}) async-start(s8[12582912]{0:T(1024)(128)(4,1)} %bitcast.446), calls=%async_computation.14 | async-start | bytes 8388608 | tf_op jit(solution)/shard_map/while
  753.0 33.3 %all-to-all-start.3 = ((bf16[4,512,3,192]{1,3,2,0:T(8,128)(2,1)}), bf16[4,512,3,192]{1,3,2,0:T(8,128)(2,1)}, u32[]{:S(2)}, u32[]{:S(2)}) async-start(bf16[4,512,3,192]{1,3,2,0:T(8,128)(2,1)} %pad_maximum_fusion.9), calls=%async_computation.3 | async-start | bytes 4718592 | tf_op jit(solution)/shard_map/while/body/eval_jaxpr/all_to_all | solution.py:15
  806.5 242.4 %reduce-scatter.6.cloned.1.call-start = ((), (), s32[]{:S(2)}) async-start(), calls=%async_computation.8 | async-start | bytes 9732096 | tf_op jit(solution)/shard_map/reduce_scatter | solution.py:272
  827.2 362.9 %reduce-scatter.10.cloned.1.call-start = ((), (), s32[]{:S(2)}) async-start(), calls=%async_computation.10 | async-start | bytes 9732096 | tf_op jit(solution)/shard_map/reduce_scatter | solution.py:277
  827.9 504.0 %reduce-scatter.12.cloned.1.call-start = ((), (), s32[]{:S(2)}) async-start(), calls=%async_computation.11 | async-start | bytes 9732096 | tf_op jit(solution)/shard_map/reduce_scatter | solution.py:279
  828.0 504.0 %copy-start.1 = (bf16[3,3,768]{2,1,0:T(4,128)(2,1)S(1)}, bf16[3,3,768]{2,1,0:T(4,128)(2,1)}, u32[]{:S(2)}) copy-start(bf16[3,3,768]{2,1,0:T(4,128)(2,1)} %param.22) | copy-start | bytes 41476
  (150 other events, 793.6 us)
Sparse Core Ops, SparseCore 0:
  806.7 100.0 reduce-scatter.7
  914.3 134.6 reduce-scatter.5
  1055.4 134.6 reduce-scatter.9
  1197.4 134.4 reduce-scatter.11
